TPU v7x, 256 devices: a whole 4x4x8 slice. The times are simulated.
256 devices in a mesh: tile: 32 (over z, x_hi, core), group: 8 (over y, x_lo).
Axes of the slice: x: 4 (x_hi: 2, x_lo: 2; x = x_hi * 2 + x_lo), y: 4, z: 8, core: 2. Of those that a mesh axis runs over, the one named last changes fastest.
Arguments:
- object_field: float32 [2, 320, 4096], P(None, 'group', 'tile'), may hold values from -6 to 6
- probe_field: float32 [2, 256, 256], replicated, may hold values from -6 to 6
- amplitudes: float32 [256, 256, 256], P(('tile', 'group')), may hold values from 0 to 4
- row_start: int32 [256], P(('tile', 'group')), may hold values from 0 to 64
- column_start: int32 [256], P(('tile', 'group')), may hold values from 0 to 128
- live_slots: int32 [256], P(('tile', 'group')), may hold values 0 or 1
Outputs:
- new_object: float32 [2, 320, 4096], P(None, 'group', 'tile')
- new_probe: float32 [2, 256, 256], replicated
All inputs are finite; a program needn't handle non-finite values. No bound on the sum of `live_slots` on one device may be relied on, other than what follows from the above.
Results may differ from a plain program's by a relative error of at most 0.0001.
Values sent between devices are 32-bit elements; how exact they have to be, the bound alone decides.
No kernel may reach another device: no remote copies, remote signals or barrier semaphores. Data moves between devices by JAX's collectives and lax.ppermute only.
A program may use at most 64 MiB of HBM per device.

v0:
```python
import math
import jax
import jax.numpy as jnp
from jax import lax
from jax.sharding import PartitionSpec as P

WIN = 256
HALO = 128


def padded_2(value, sides, width):
    for axis, dim in sides:
        count, length = (lax.axis_size(axis), value.shape[dim])
        up = [(i, (i + 1) % count) for i in range(count - 1)]
        down = [(j, i) for i, j in up]
        last = lax.slice_in_dim(value, length - width, length, axis=dim)
        initial = lax.slice_in_dim(value, 0, width, axis=dim)
        before = lax.ppermute(last, axis, up)
        after = lax.ppermute(initial, axis, down)
        value = jnp.concatenate([before, value, after], axis=dim)
    return value


def dft_tables(length):
    counter = jnp.arange(length, dtype=jnp.int32)
    product = counter[:, None] * counter[None, :] % length
    angles = 2.0 * math.pi / length * product.astype(jnp.float32)
    factor = 1.0 / math.sqrt(length)
    return (jnp.cos(angles) * factor, jnp.sin(angles) * factor)


def apply_left(matrix, values):
    return jnp.einsum("jk,pkl->pjl", matrix, values, precision=lax.Precision.HIGHEST)


def apply_right(values, matrix):
    return jnp.einsum("pjk,kl->pjl", values, matrix, precision=lax.Precision.HIGHEST)


def transform(real_part, imag_part, cos_table, sin_table, sign):
    left_real = apply_left(cos_table, real_part) - sign * apply_left(sin_table, imag_part)
    left_imag = apply_left(cos_table, imag_part) + sign * apply_left(sin_table, real_part)
    right_real = apply_right(left_real, cos_table) - sign * apply_right(left_imag, sin_table)
    right_imag = apply_right(left_imag, cos_table) + sign * apply_right(left_real, sin_table)
    return (right_real, right_imag)


def window_terms(windows, probe_field, amplitudes, live_slots, cos_table, sin_table):
    sample_real = windows[:, 0]
    sample_imag = windows[:, 1]
    probe_real = probe_field[0]
    probe_imag = probe_field[1]
    exit_real = probe_real * sample_real - probe_imag * sample_imag
    exit_imag = probe_real * sample_imag + probe_imag * sample_real
    far_real, far_imag = transform(exit_real, exit_imag, cos_table, sin_table, -1.0)
    modulus = jnp.maximum(jnp.sqrt(far_real * far_real + far_imag * far_imag), 0.25)
    factor = 1.0 - amplitudes / modulus
    miss_real, miss_imag = transform(
        far_real * factor, far_imag * factor, cos_table, sin_table, 1.0
    )
    weight = live_slots.astype(jnp.float32)[:, None, None]
    miss_real = miss_real * weight
    miss_imag = miss_imag * weight
    grad_real = probe_real * miss_real + probe_imag * miss_imag
    grad_imag = probe_real * miss_imag - probe_imag * miss_real
    probe_light = weight * (probe_real * probe_real + probe_imag * probe_imag)
    terms = jnp.stack([grad_real, grad_imag, probe_light], axis=1)
    probe_grad = jnp.stack(
        [
            jnp.sum(sample_real * miss_real + sample_imag * miss_imag, axis=0),
            jnp.sum(sample_real * miss_imag - sample_imag * miss_real, axis=0),
        ],
        axis=0,
    )
    window_light = jnp.sum(weight * (sample_real * sample_real + sample_imag * sample_imag), axis=0)
    return (terms, probe_grad, window_light)


def add_windows(accum, terms, top_rows, left_edges):
    zero_index = jnp.zeros((), jnp.int32)
    channels = terms.shape[1]

    def place(slot, current):
        corner = (zero_index, top_rows[slot], left_edges[slot])
        piece = lax.dynamic_slice(current, corner, (channels, WIN, WIN))
        return lax.dynamic_update_slice(current, piece + terms[slot], corner)

    return lax.fori_loop(0, terms.shape[0], place, accum)


def cut_windows(padded, top_rows, left_edges):
    zero_index = jnp.zeros((), jnp.int32)

    def single(top_row, left_edge):
        return lax.dynamic_slice(padded, (zero_index, top_row, left_edge), (2, WIN, WIN))

    return jax.vmap(single)(top_rows, left_edges)


def edge_strips(accum):
    return jnp.concatenate([accum[:, :, :HALO], accum[:, :, accum.shape[2] - HALO :]], axis=2)


def add_edges(inner, arrived):
    width = inner.shape[2]
    inner = inner.at[:, :, :HALO].add(arrived[:, :, :HALO])
    return inner.at[:, :, width - HALO :].add(arrived[:, :, arrived.shape[2] - HALO :])


def apply_updates(object_field, probe_field, share, probe_grad, window_light):
    light_max = jnp.max(probe_field[0] * probe_field[0] + probe_field[1] * probe_field[1]) + 1e-06
    new_object = object_field - share[0:2] / (share[2:3] + 0.25 * light_max)
    new_probe = (
        probe_field - probe_grad / (window_light + 0.25 * jnp.mean(window_light) + 1e-05)[None]
    )
    return (new_object, new_probe)


def local(object_field, probe_field, amplitudes, row_start, column_start, live_slots):
    cos_table, sin_table = dft_tables(WIN)
    full_rows = lax.all_gather(object_field, "group", axis=1, tiled=True)
    padded = padded_2(full_rows, (("tile", 2),), HALO)
    windows = cut_windows(padded, row_start, column_start)
    terms, probe_grad, window_light = window_terms(
        windows, probe_field, amplitudes, live_slots, cos_table, sin_table
    )
    accum = jnp.zeros((terms.shape[1], padded.shape[1], padded.shape[2]), jnp.float32)
    accum = add_windows(accum, terms, row_start, column_start)
    arrived = padded_2(edge_strips(accum), (("tile", 2),), HALO)
    summed = add_edges(accum[:, :, HALO : accum.shape[2] - HALO], arrived)
    share = lax.psum_scatter(summed, "group", scatter_dimension=1, tiled=True)
    probe_grad, window_light = lax.psum((probe_grad, window_light), ("tile", "group"))
    object_field, probe_field = apply_updates(
        object_field, probe_field, share, probe_grad, window_light
    )
    return (object_field, probe_field)


def solution(mesh):
    return jax.shard_map(
        local,
        mesh=mesh,
        in_specs=(
            P(None, "group", "tile"),
            P(),
            P(("tile", "group"), None, None),
            P(("tile", "group")),
            P(("tile", "group")),
            P(("tile", "group")),
        ),
        out_specs=(P(None, "group", "tile"), P()),
        check_vma=False,
    )
```

profile of v0, /device:TPU:2, one launch (start us, length us, event | category | flops | bytes accessed | tf_op | source)
XLA Modules:
  0.0 370.7 jit_solution(3378128131235949026)
XLA Ops:
  8.0 0.0 all-reduce.3.cloned.1.call-start
  8.1 29.8 %all_gather.3 = f32[2,320,128]{2,1,0:T(8,128)S(1)} all-gather(f32[2,40,128]{2,1,0:T(8,128)} %param.14), channel_id=1, replica_groups=mesh['tile'=32,'group'=8] {'group'}, dimensions={1}, use_global_device_ids=true | all-gather | bytes 368640 | tf_op jit(solution)/shard_map/all_gather | solution.py:121
  37.9 1.3 collective-permute-start.1
  39.2 3.1 collective-permute-start
  44.2 0.0 collective-permute-done.1
  44.2 0.0 collective-permute-done
  44.2 0.4 fusion.12
  44.6 0.1 fusion.40
  44.7 1.5 fusion.38
  46.2 1.5 fusion.34
  47.7 1.5 fusion.9
  49.2 1.5 fusion.7
  50.7 1.5 fusion.47
  52.1 0.0 copy-start.6
  52.2 1.5 fusion.48
  53.6 1.5 fusion.4
  55.1 1.7 bitcast_multiply_fusion.11
  56.9 1.5 fusion.31
  58.4 1.5 fusion.27
  59.8 1.5 fusion.3
  61.3 1.5 fusion.2
  62.8 1.5 fusion.45
  64.3 1.5 fusion.46
  65.8 1.5 fusion
  67.3 0.0 copy-start.1
  67.3 1.7 fusion.1
  69.0 0.7 fusion.24
  69.7 0.1 maximum_bitcast_fusion
  69.8 0.1 broadcast_in_dim.6
  69.9 10.9 %dynamic_update_slice.4 = f32[3,320,384]{2,1,0:T(8,128)S(1)} dynamic-update-slice(f32[3,320,384]{2,1,0:T(8,128)S(1)} %broadcast_in_dim.6, f32[3,256,256]{2,1,0:T(8,128)S(1)} %maximum_bitcast_fusion, s32[]{:T(128)} %constant.112.clone.1, s32[]{:T(128)S(6)} %select_n.60, s32[]{:T(128)S(6)} %select_n.61) | dynamic-update-slice | bytes 1572868 | tf_op jit(solution)/shard_map/while/body/eval_jaxpr/dynamic_update_slice | solution.py:86
  80.8 0.0 copy-start.2
  80.8 0.9 fusion.132
  81.6 6.6 %collective-permute-start.2 = (f32[3,320,128]{2,1,0:T(8,128)}, f32[3,320,128]{2,1,0:T(8,128)S(1)}, u32[]{:S(2)}, u32[]{:S(2)}) collective-permute-start(f32[3,320,128]{2,1,0:T(8,128)} %get-tuple-element.73), channel_id=1, source_target_pairs={{0,8},{8,16},{16,24},{24,32},{32,40},{40,48},{48,56},{56,64},{64,7... | collective-permute-start | bytes 1474568 | tf_op jit(solution)/shard_map/ppermute | solution.py:18
  88.2 1.3 collective-permute-start.3
  89.6 0.8 fusion.18
  90.4 0.8 pad_maximum_fusion
  91.2 0.0 all-reduce.3.cloned.1.call-update
  91.2 0.0 reduce-scatter.2.cloned.1.call-start
  91.3 0.0 collective-permute-done.2
  91.3 4.5 %collective-permute-done.3 = f32[3,320,128]{2,1,0:T(8,128)} collective-permute-done((f32[3,320,128]{2,1,0:T(8,128)S(1)}, f32[3,320,128]{2,1,0:T(8,128)}, u32[]{:S(2)}, u32[]{:S(2)}) %collective-permute-start.3) | collective-permute-done | bytes 491552 | tf_op jit(solution)/shard_map/ppermute | solution.py:19
  95.7 1.9 fusion.13
  97.6 0.0 reduce-scatter.2.cloned.1.call-update
  98.3 257.6 %all-reduce.3.cloned.1.call-done = (f32[2,256,256]{2,1,0:T(8,128)}, f32[256,256]{1,0:T(8,128)}) async-done(((f32[2,256,256]{2,1,0:T(8,128)}, f32[256,256]{1,0:T(8,128)}), (f32[2,256,256]{2,1,0:T(8,128)}, f32[256,256]{1,0:T(8,128)})) %all-reduce.3.cloned.1.call-update) | async-done | bytes 786448 | tf_op jit(solution)/shard_map/psum | solution.py:132
  355.9 1.6 reduce_sum.8
  358.2 1.0 add_add_fusion
  359.2 1.9 divide_subtract_fusion
  361.1 0.7 fusion.51
  361.9 1.4 fusion.50
  (12 shorter events, 0.0 us)
Async XLA Ops:
  8.0 36.6 %copy-start = (f32[2,256,256]{2,1,0:T(8,128)S(1)}, f32[2,256,256]{2,1,0:T(8,128)}, u32[]{:S(2)}) copy-start(f32[2,256,256]{2,1,0:T(8,128)} %param.15) | copy-start | bytes 1572868
  8.0 347.9 %all-reduce.3.cloned.1.call-start = ((), (), s32[]{:S(2)}) async-start(), calls=%async_computation.2 | async-start | bytes 1572864 | tf_op jit(solution)/shard_map/psum | solution.py:132
  37.9 6.3 %collective-permute-start.1 = (f32[2,320,128]{2,1,0:T(8,128)S(1)}, f32[2,320,128]{2,1,0:T(8,128)S(1)}, u32[]{:S(2)}, u32[]{:S(2)}) collective-permute-start(f32[2,320,128]{2,1,0:T(8,128)S(1)} %all_gather.3), channel_id=1, source_target_pairs={{8,0},{16,8},{24,16},{32,24},{40,32},{48,40},{56,48},{64,56},{72,6... | collective-permute-start | bytes 983048 | tf_op jit(solution)/shard_map/ppermute | solution.py:19
  39.2 5.0 %collective-permute-start = (f32[2,320,128]{2,1,0:T(8,128)S(1)}, f32[2,320,128]{2,1,0:T(8,128)S(1)}, u32[]{:S(2)}, u32[]{:S(2)}) collective-permute-start(f32[2,320,128]{2,1,0:T(8,128)S(1)} %all_gather.3), channel_id=1, source_target_pairs={{0,8},{8,16},{16,24},{24,32},{32,40},{40,48},{48,56},{56,64},{64,7... | collective-permute-start | bytes 983048 | tf_op jit(solution)/shard_map/ppermute | solution.py:18
  52.1 3.0 copy-start.6
  67.3 2.4 copy-start.1
  69.0 0.8 copy-start.3
  80.8 8.8 %copy-start.2 = (f32[256,256]{1,0:T(8,128)S(1)}, f32[256,256]{1,0:T(8,128)}, u32[]{:S(2)}) copy-start(f32[256,256]{1,0:T(8,128)} %copy-done.1) | copy-start | bytes 786436
  80.8 8.8 %copy-start.4 = (f32[256,256]{1,0:T(8,128)S(1)}, f32[256,256]{1,0:T(8,128)}, u32[]{:S(2)}) copy-start(f32[256,256]{1,0:T(8,128)} %copy-done.3) | copy-start | bytes 786436
  81.6 9.6 %collective-permute-start.2 = (f32[3,320,128]{2,1,0:T(8,128)}, f32[3,320,128]{2,1,0:T(8,128)S(1)}, u32[]{:S(2)}, u32[]{:S(2)}) collective-permute-start(f32[3,320,128]{2,1,0:T(8,128)} %get-tuple-element.73), channel_id=1, source_target_pairs={{0,8},{8,16},{16,24},{24,32},{32,40},{40,48},{48,56},{56,64},{64,7... | collective-permute-start | bytes 1474568 | tf_op jit(solution)/shard_map/ppermute | solution.py:18
  88.2 7.5 %collective-permute-start.3 = (f32[3,320,128]{2,1,0:T(8,128)S(1)}, f32[3,320,128]{2,1,0:T(8,128)}, u32[]{:S(2)}, u32[]{:S(2)}) collective-permute-start(f32[3,320,128]{2,1,0:T(8,128)S(1)} %get-tuple-element.74), channel_id=1, source_target_pairs={{8,0},{16,8},{24,16},{32,24},{40,32},{48,40},{56,48},{64,56},{72,6... | collective-permute-start | bytes 1474568 | tf_op jit(solution)/shard_map/ppermute | solution.py:19
  91.2 269.9 %reduce-scatter.2.cloned.1.call-start = ((), (), s32[]{:S(2)}) async-start(), calls=%async_computation.1 | async-start | bytes 552960 | tf_op jit(solution)/shard_map/reduce_scatter | solution.py:131
  97.6 264.2 %copy-start.5 = (f32[2,40,128]{2,1,0:T(8,128)S(1)}, f32[2,40,128]{2,1,0:T(8,128)}, u32[]{:S(2)}) copy-start(f32[2,40,128]{2,1,0:T(8,128)} %param.14) | copy-start | bytes 122884
Sparse Core Ops, SparseCore 0:
  91.3 264.5 all-reduce.2
Sparse Core Ops, SparseCore 1:
  97.8 51.0 reduce-scatter.1
where the time goes:
time: 371 us
  waiting for transfers between devices  262 us (71%)
  blocking collectives  29.8 us (8%)
  matrix products  24.1 us (6%)
  between operations  19 us (5%)
  starting transfers between devices  12.3 us (3%)
  local copies, waits for them, and re-layouts  11.9 us (3%)
  other arithmetic  11.4 us (3%)
    psum x1, waiting for transfers between devices, local(): lax.psum((probe_grad, window_light), ('tile', 'group'))  258 us
    all_gather x1, blocking collectives, local(): full_rows = lax.all_gather(object_field, 'group', axis=1, tiled=True)  29.8 us
    dot_general x8, matrix products, apply_right(): jnp.einsum('pjk,kl->pjl', values, matrix, precision=lax.Precision.HIGHEST)  12.3 us
    dot_general x8, matrix products, apply_left(): jnp.einsum('jk,pkl->pjl', matrix, values, precision=lax.Precision.HIGHEST)  11.8 us
    dynamic_update_slice x1, local copies, waits for them, and re-layouts, place(): return lax.dynamic_update_slice(current, piece + terms[slot], corner)  10.9 us
    ppermute x2, starting transfers between devices, padded_2(): before = lax.ppermute(last, axis, up)  9.64 us
  transfers between devices with their start and end apart: 6, of which 2 were waited for; matrix products, arithmetic and copies ran while one was open for 2% of the time, Pallas kernels for 0%

commit v1 on v0

--- a/solution.py
+++ b/solution.py
@@ -118,7 +118,9 @@
 
 def local(object_field, probe_field, amplitudes, row_start, column_start, live_slots):
     cos_table, sin_table = dft_tables(WIN)
-    full_rows = lax.all_gather(object_field, "group", axis=1, tiled=True)
+    full_rows = jnp.concatenate(
+        lax.all_to_all(jnp.stack([object_field] * lax.axis_size("group")), "group", 0, 0), axis=1
+    )
     padded = padded_2(full_rows, (("tile", 2),), HALO)
     windows = cut_windows(padded, row_start, column_start)
     terms, probe_grad, window_light = window_terms(

time: 371 us -> 354 us (0.954)
  blocking collectives: 29.8 us -> 12.7 us
    all_gather x1 -> x0, blocking collectives: 29.8 us -> none  [local(): full_rows = lax.all_gather(object_field, 'group', axis=1, tiled=True)]
    all_to_all x0 -> x1, blocking collectives: none -> 12.7 us  [local(): lax.all_to_all(jnp.stack([object_field] * lax.axis_size('group')), 'group...]
where the time goes in v1:
time: 354 us
  waiting for transfers between devices  261 us (74%)
  matrix products  24.1 us (7%)
  between operations  19 us (5%)
  local copies, waits for them, and re-layouts  12.7 us (4%)
  blocking collectives  12.7 us (4%)
  starting transfers between devices  12.3 us (3%)
  other arithmetic  11.4 us (3%)
    psum x1, waiting for transfers between devices, local(): lax.psum((probe_grad, window_light), ('tile', 'group'))  257 us
    all_to_all x1, blocking collectives, local(): lax.all_to_all(jnp.stack([object_field] * lax.axis_size('group')), 'group...  12.7 us
    dot_general x8, matrix products, apply_right(): jnp.einsum('pjk,kl->pjl', values, matrix, precision=lax.Precision.HIGHEST)  12.3 us
    dot_general x8, matrix products, apply_left(): jnp.einsum('jk,pkl->pjl', matrix, values, precision=lax.Precision.HIGHEST)  11.8 us
    dynamic_update_slice x1, local copies, waits for them, and re-layouts, place(): return lax.dynamic_update_slice(current, piece + terms[slot], corner)  10.9 us
    ppermute x2, starting transfers between devices, padded_2(): before = lax.ppermute(last, axis, up)  9.62 us
  transfers between devices with their start and end apart: 6, of which 2 were waited for; matrix products, arithmetic and copies ran while one was open for 2% of the time, Pallas kernels for 0%

profile of v1, /device:TPU:2, one launch (start us, length us, event | category | flops | bytes accessed | tf_op | source)
XLA Modules:
  0.0 353.7 jit_solution(11822167341686070802)
XLA Ops:
  8.0 0.0 all-reduce.3.cloned.1.call-start
  8.0 0.8 stack.12
  8.8 0.0 copy-start
  8.9 12.7 %all_to_all.5 = f32[8,2,40,128]{3,2,1,0:T(8,128)S(1)} all-to-all(f32[8,2,40,128]{3,2,1,0:T(8,128)S(1)} %stack.12), channel_id=1, replica_groups=mesh['tile'=32,'group'=8] {'group'}, dimensions={0} | all-to-all | bytes 655360 | tf_op jit(solution)/shard_map/all_to_all | solution.py:122
  21.6 1.3 collective-permute-start.1
  22.9 3.1 collective-permute-start
  27.9 0.0 collective-permute-done.1
  27.9 0.4 fusion.12
  28.3 0.1 fusion.40
  28.4 1.5 fusion.38
  29.9 1.5 fusion.34
  31.4 1.5 fusion.9
  32.9 1.5 fusion.7
  34.4 1.5 fusion.47
  35.8 0.0 copy-start.6
  35.9 1.5 fusion.48
  37.3 1.5 fusion.4
  38.8 1.7 bitcast_multiply_fusion.11
  40.6 1.5 fusion.31
  42.1 1.5 fusion.27
  43.5 1.5 fusion.3
  45.0 1.5 fusion.2
  46.5 1.5 fusion.45
  48.0 1.5 fusion.46
  49.5 1.5 fusion
  51.0 0.0 copy-start.1
  51.0 1.7 fusion.1
  52.7 0.7 fusion.24
  53.4 0.1 maximum_bitcast_fusion
  53.5 0.1 broadcast_in_dim.6
  53.6 10.9 %dynamic_update_slice.4 = f32[3,320,384]{2,1,0:T(8,128)S(1)} dynamic-update-slice(f32[3,320,384]{2,1,0:T(8,128)S(1)} %broadcast_in_dim.6, f32[3,256,256]{2,1,0:T(8,128)S(1)} %maximum_bitcast_fusion, s32[]{:T(128)} %constant.112.clone.1, s32[]{:T(128)S(6)} %select_n.60, s32[]{:T(128)S(6)} %select_n.61) | dynamic-update-slice | bytes 1572868 | tf_op jit(solution)/shard_map/while/body/eval_jaxpr/dynamic_update_slice | solution.py:86
  64.5 0.0 copy-start.2
  64.5 0.9 fusion.132
  65.4 6.6 %collective-permute-start.2 = (f32[3,320,128]{2,1,0:T(8,128)}, f32[3,320,128]{2,1,0:T(8,128)S(1)}, u32[]{:S(2)}, u32[]{:S(2)}) collective-permute-start(f32[3,320,128]{2,1,0:T(8,128)} %get-tuple-element.73), channel_id=1, source_target_pairs={{0,8},{8,16},{16,24},{24,32},{32,40},{40,48},{48,56},{56,64},{64,7... | collective-permute-start | bytes 1474568 | tf_op jit(solution)/shard_map/ppermute | solution.py:18
  71.9 1.3 collective-permute-start.3
  73.2 0.8 fusion.18
  74.0 0.8 pad_maximum_fusion
  74.9 0.0 all-reduce.3.cloned.1.call-update
  74.9 0.0 reduce-scatter.2.cloned.1.call-start
  74.9 4.5 %collective-permute-done.3 = f32[3,320,128]{2,1,0:T(8,128)} collective-permute-done((f32[3,320,128]{2,1,0:T(8,128)S(1)}, f32[3,320,128]{2,1,0:T(8,128)}, u32[]{:S(2)}, u32[]{:S(2)}) %collective-permute-start.3) | collective-permute-done | bytes 491552 | tf_op jit(solution)/shard_map/ppermute | solution.py:19
  79.4 1.9 fusion.13
  81.3 0.0 reduce-scatter.2.cloned.1.call-update
  82.0 256.9 %all-reduce.3.cloned.1.call-done = (f32[2,256,256]{2,1,0:T(8,128)}, f32[256,256]{1,0:T(8,128)}) async-done(((f32[2,256,256]{2,1,0:T(8,128)}, f32[256,256]{1,0:T(8,128)}), (f32[2,256,256]{2,1,0:T(8,128)}, f32[256,256]{1,0:T(8,128)})) %all-reduce.3.cloned.1.call-update) | async-done | bytes 786448 | tf_op jit(solution)/shard_map/psum | solution.py:134
  338.9 1.6 reduce_sum.8
  341.2 1.0 add_add_fusion
  342.2 1.9 divide_subtract_fusion
  344.1 0.7 fusion.51
  344.8 1.4 fusion.50
  (14 shorter events, 0.0 us)
Async XLA Ops:
  8.0 330.9 %all-reduce.3.cloned.1.call-start = ((), (), s32[]{:S(2)}) async-start(), calls=%async_computation.3 | async-start | bytes 1572864 | tf_op jit(solution)/shard_map/psum | solution.py:134
  8.8 19.5 %copy-start = (f32[2,256,256]{2,1,0:T(8,128)S(1)}, f32[2,256,256]{2,1,0:T(8,128)}, u32[]{:S(2)}) copy-start(f32[2,256,256]{2,1,0:T(8,128)} %param.15) | copy-start | bytes 1572868
  21.6 6.3 %collective-permute-start.1 = (f32[2,320,128]{2,1,0:T(8,128)S(1)}, f32[2,320,128]{2,1,0:T(8,128)S(1)}, u32[]{:S(2)}, u32[]{:S(2)}) collective-permute-start(f32[2,320,128]{2,1,0:T(8,128)S(1)} %bitcast.152), channel_id=1, source_target_pairs={{8,0},{16,8},{24,16},{32,24},{40,32},{48,40},{56,48},{64,56},{72,6... | collective-permute-start | bytes 983048 | tf_op jit(solution)/shard_map/ppermute | solution.py:19
  22.9 5.0 %collective-permute-start = (f32[2,320,128]{2,1,0:T(8,128)S(1)}, f32[2,320,128]{2,1,0:T(8,128)S(1)}, u32[]{:S(2)}, u32[]{:S(2)}) collective-permute-start(f32[2,320,128]{2,1,0:T(8,128)S(1)} %bitcast.153), channel_id=1, source_target_pairs={{0,8},{8,16},{16,24},{24,32},{32,40},{40,48},{48,56},{56,64},{64,7... | collective-permute-start | bytes 983048 | tf_op jit(solution)/shard_map/ppermute | solution.py:18
  35.8 3.0 copy-start.6
  51.0 2.4 copy-start.1
  52.7 0.8 copy-start.3
  64.5 8.8 %copy-start.2 = (f32[256,256]{1,0:T(8,128)S(1)}, f32[256,256]{1,0:T(8,128)}, u32[]{:S(2)}) copy-start(f32[256,256]{1,0:T(8,128)} %copy-done.1) | copy-start | bytes 786436
  64.5 8.8 %copy-start.4 = (f32[256,256]{1,0:T(8,128)S(1)}, f32[256,256]{1,0:T(8,128)}, u32[]{:S(2)}) copy-start(f32[256,256]{1,0:T(8,128)} %copy-done.3) | copy-start | bytes 786436
  65.4 9.6 %collective-permute-start.2 = (f32[3,320,128]{2,1,0:T(8,128)}, f32[3,320,128]{2,1,0:T(8,128)S(1)}, u32[]{:S(2)}, u32[]{:S(2)}) collective-permute-start(f32[3,320,128]{2,1,0:T(8,128)} %get-tuple-element.73), channel_id=1, source_target_pairs={{0,8},{8,16},{16,24},{24,32},{32,40},{40,48},{48,56},{56,64},{64,7... | collective-permute-start | bytes 1474568 | tf_op jit(solution)/shard_map/ppermute | solution.py:18
  71.9 7.5 %collective-permute-start.3 = (f32[3,320,128]{2,1,0:T(8,128)S(1)}, f32[3,320,128]{2,1,0:T(8,128)}, u32[]{:S(2)}, u32[]{:S(2)}) collective-permute-start(f32[3,320,128]{2,1,0:T(8,128)S(1)} %get-tuple-element.74), channel_id=1, source_target_pairs={{8,0},{16,8},{24,16},{32,24},{40,32},{48,40},{56,48},{64,56},{72,6... | collective-permute-start | bytes 1474568 | tf_op jit(solution)/shard_map/ppermute | solution.py:19
  74.9 269.2 %reduce-scatter.2.cloned.1.call-start = ((), (), s32[]{:S(2)}) async-start(), calls=%async_computation.2 | async-start | bytes 552960 | tf_op jit(solution)/shard_map/reduce_scatter | solution.py:133
  81.3 263.5 %copy-start.5 = (f32[2,40,128]{2,1,0:T(8,128)S(1)}, f32[2,40,128]{2,1,0:T(8,128)}, u32[]{:S(2)}) copy-start(f32[2,40,128]{2,1,0:T(8,128)} %param.14) | copy-start | bytes 122884
Sparse Core Ops, SparseCore 0:
  75.0 263.8 all-reduce.2
Sparse Core Ops, SparseCore 1:
  81.4 50.2 reduce-scatter.1
